TPU v7x, 512 devices: a whole 4x8x8 slice. The times are simulated.
512 devices in a mesh: gx: 8 (over z), gy: 8 (over y_lo, core), gz: 8 (over y_hi, x).
Axes of the slice: x: 4, y: 8 (y_hi: 2, y_lo: 4; y = y_hi * 4 + y_lo), z: 8, core: 2. Of those that a mesh axis runs over, the one named last changes fastest.
Arguments:
- x_in: bfloat16 [3072, 5120], P(('gy', 'gx'), 'gz'), may hold values from -190 to 190
- gain: float32 [5120], P('gz'), may hold values from 0.25 to 1.75
- w_up: bfloat16 [5120, 7168], P(('gz', 'gy'), 'gx'), may hold values from -0.078125 to 0.078125
- w_down: bfloat16 [7168, 5120], P(('gx', 'gy'), 'gz'), may hold values from -0.0625 to 0.0625
- d_out: bfloat16 [3072, 5120], P(('gy', 'gx'), 'gz'), may hold values from -1.1953125 to 1.1953125
Outputs:
- d_x: bfloat16 [3072, 5120], P(('gy', 'gx'), 'gz')
- d_w_up: bfloat16 [5120, 7168], P(('gz', 'gy'), 'gx')
- d_w_down: bfloat16 [7168, 5120], P(('gx', 'gy'), 'gz')
- d_gain: float32 [5120], P('gz')
All inputs are finite; a program needn't handle non-finite values.
Results may differ from a plain program's by a relative error of at most 0.02.
Values may be sent and summed in bfloat16 or wider, within the bound.
No kernel may reach another device: no remote copies, remote signals or barrier semaphores. Data moves between devices by JAX's collectives and lax.ppermute only.
A program may use at most 64 MiB of HBM per device.

v0:
```python
import jax
import jax.numpy as jnp
from jax import lax
from jax.sharding import PartitionSpec as P


def gelu_pair(hidden):
    cdf = 0.5 * (1.0 + jax.scipy.special.erf(hidden * 0.7071067811865476))
    slope = cdf + hidden * jnp.exp(-0.5 * hidden * hidden) * 0.3989422804014327
    return (hidden * cdf, slope)


def body(x_in, gain, w_up, w_down, d_out):
    width = x_in.shape[1] * lax.axis_size("gz")
    xf = x_in.astype(jnp.float32)
    total = lax.psum(jnp.sum(xf, axis=1), "gz")
    mean = total / width
    centered = xf - mean[:, None]
    var = lax.psum(jnp.sum(centered * centered, axis=1), "gz") / width
    inv = lax.rsqrt(var + 1e-05)[:, None]
    normed = centered * inv
    z_local = (normed * gain).astype(jnp.bfloat16)
    up_full = lax.all_gather(w_up, "gy", axis=0, tiled=True)
    z_rows = lax.all_gather(z_local, "gx", axis=0, tiled=True)
    part_rows = z_rows
    hidden = lax.psum_scatter(
        jnp.dot(part_rows, up_full, preferred_element_type=jnp.float32).astype(jnp.bfloat16),
        "gz",
        scatter_dimension=0,
        tiled=True,
    ).astype(jnp.float32)
    act_f, slope = gelu_pair(hidden)
    act = act_f.astype(jnp.bfloat16)
    down_full = lax.all_gather(w_down, "gy", axis=0, tiled=True)
    out_rows = lax.all_gather(d_out, "gx", axis=0, tiled=True)
    act_rows = lax.all_gather(act, "gz", axis=0, tiled=True)
    part_rows = out_rows
    d_act = lax.psum_scatter(
        lax.dot_general(
            part_rows, down_full, (((1,), (1,)), ((), ())), preferred_element_type=jnp.float32
        ).astype(jnp.bfloat16),
        "gz",
        scatter_dimension=0,
        tiled=True,
    ).astype(jnp.float32)
    d_hidden = (d_act * slope).astype(jnp.bfloat16)
    hgrad_rows = lax.all_gather(d_hidden, "gz", axis=0, tiled=True)
    columns = act_rows
    d_w_down = lax.psum_scatter(
        lax.dot_general(
            columns, out_rows, (((0,), (0,)), ((), ())), preferred_element_type=jnp.float32
        ).astype(jnp.bfloat16),
        "gy",
        scatter_dimension=0,
        tiled=True,
    )
    columns = z_rows
    d_w_up = lax.psum_scatter(
        lax.dot_general(
            columns, hgrad_rows, (((0,), (0,)), ((), ())), preferred_element_type=jnp.float32
        ).astype(jnp.bfloat16),
        "gy",
        scatter_dimension=0,
        tiled=True,
    )
    part_rows = hgrad_rows
    d_z = lax.psum_scatter(
        lax.dot_general(
            part_rows, up_full, (((1,), (1,)), ((), ())), preferred_element_type=jnp.float32
        ).astype(jnp.bfloat16),
        "gx",
        scatter_dimension=0,
        tiled=True,
    ).astype(jnp.float32)
    d_gain = lax.psum(jnp.sum(d_z * normed, axis=0), ("gx", "gy"))
    d_scaled = d_z * gain
    scaled_sum, cross_sum = lax.psum(
        (jnp.sum(d_scaled, axis=1), jnp.sum(d_scaled * normed, axis=1)), "gz"
    )
    d_x = inv * (d_scaled - scaled_sum[:, None] / width - normed * (cross_sum[:, None] / width))
    return (d_x.astype(jnp.bfloat16), d_w_up, d_w_down, d_gain)


def solution(mesh):
    placed = (
        P(("gy", "gx"), "gz"),
        P("gz"),
        P(("gz", "gy"), "gx"),
        P(("gx", "gy"), "gz"),
        P(("gy", "gx"), "gz"),
    )
    return jax.shard_map(
        body,
        mesh=mesh,
        in_specs=placed,
        out_specs=(P(("gy", "gx"), "gz"), P(("gz", "gy"), "gx"), P(("gx", "gy"), "gz"), P("gz")),
        check_vma=False,
    )
```

profile of v0, /device:TPU:1, one launch (start us, length us, event | category | flops | bytes accessed | tf_op | source)
XLA Modules:
  0.0 543.6 jit_solution(16610349977316155122)
XLA Ops:
  7.2 0.7 all-gather.3.cloned.1.call-update
  7.9 0.7 all-gather.5.cloned.1.call-update
  8.7 27.0 %all_gather.18 = bf16[384,640]{1,0:T(8,128)(2,1)S(1)} all-gather(bf16[48,640]{1,0:T(8,128)(2,1)} %param.9), channel_id=1, replica_groups=mesh['gx'=8,'gy'=8,'gz'=8] {'gx'}, dimensions={0}, use_global_device_ids=true | all-gather | bytes 552960 | tf_op jit(solution)/shard_map/all_gather | solution.py:35
  35.7 17.8 %all-gather.3.cloned.1.call-done = bf16[896,640]{1,0:T(8,128)(2,1)} async-done(((bf16[112,640]{1,0:T(8,128)(2,1)}), bf16[896,640]{1,0:T(8,128)(2,1)}) %all-gather.3.cloned.1.call-update) | async-done | bytes 1146896 | tf_op jit(solution)/shard_map/all_gather | solution.py:34
  53.5 2.9 convolution_convert_fusion.3
  56.5 0.1 convert_reduce_fusion
  56.6 26.6 %psum.35 = f32[48]{0:T(128)S(1)} all-reduce(f32[48]{0:T(128)S(1)} %convert_reduce_fusion), channel_id=1, replica_groups=mesh['gx'=8,'gy'=8,'gz'=8] {'gz'}, use_global_device_ids=true, to_apply=%region_1.0 | all-reduce | flops 48 | bytes 384 | tf_op jit(solution)/shard_map/psum | solution.py:16
  83.2 0.2 fusion.20
  83.4 20.3 %psum.36 = f32[48]{0:T(128)S(1)} all-reduce(f32[48]{0:T(128)S(1)} %fusion.20), channel_id=1, replica_groups=mesh['gx'=8,'gy'=8,'gz'=8] {'gz'}, use_global_device_ids=true, to_apply=%region_3.0 | all-reduce | flops 48 | bytes 384 | tf_op jit(solution)/shard_map/psum | solution.py:19
  103.7 0.1 fusion.16
  103.8 22.4 %all_gather.20 = bf16[384,640]{1,0:T(8,128)(2,1)S(1)} all-gather(bf16[48,640]{1,0:T(8,128)(2,1)S(1)} %fusion.16), channel_id=1, replica_groups=mesh['gx'=8,'gy'=8,'gz'=8] {'gx'}, dimensions={0}, use_global_device_ids=true | all-gather | bytes 552960 | tf_op jit(solution)/shard_map/all_gather | solution.py:24
  126.3 2.9 convolution_convert_fusion.2
  129.3 56.7 %reduce-scatter.6.cloned.1.call-done = bf16[48,896]{1,0:T(8,128)(2,1)} async-done(((bf16[384,896]{1,0:T(8,128)(2,1)}), bf16[48,896]{1,0:T(8,128)(2,1)}) %reduce-scatter.6.cloned.1.call-update) | async-done | bytes 86032 | tf_op jit(solution)/shard_map/reduce_scatter | solution.py:38
  185.9 88.3 %reduce-scatter.8.cloned.1.call-done = bf16[48,896]{1,0:T(8,128)(2,1)} async-done(((bf16[384,896]{1,0:T(8,128)(2,1)}), bf16[48,896]{1,0:T(8,128)(2,1)}) %reduce-scatter.8.cloned.1.call-update) | async-done | bytes 86032 | tf_op jit(solution)/shard_map/reduce_scatter | solution.py:26
  274.3 1.0 fusion.8
  275.3 39.4 %all_gather.22 = bf16[384,896]{1,0:T(8,128)(2,1)S(1)} all-gather(bf16[48,896]{1,0:T(8,128)(2,1)S(1)} %get-tuple-element.10), channel_id=1, replica_groups=mesh['gx'=8,'gy'=8,'gz'=8] {'gz'}, dimensions={0}, use_global_device_ids=true | all-gather | bytes 774144 | tf_op jit(solution)/shard_map/all_gather | solution.py:47
  314.7 1.6 convolution_convert_fusion.4
  316.4 41.4 %all_gather.23 = bf16[384,896]{1,0:T(8,128)(2,1)S(1)} all-gather(bf16[48,896]{1,0:T(8,128)(2,1)S(1)} %get-tuple-element.9), channel_id=1, replica_groups=mesh['gx'=8,'gy'=8,'gz'=8] {'gz'}, dimensions={0}, use_global_device_ids=true | all-gather | bytes 774144 | tf_op jit(solution)/shard_map/all_gather | solution.py:36
  357.8 1.9 convolution_convert_fusion
  359.8 1.9 convolution_convert_fusion.1
  361.7 1.0 fusion.22
  362.7 23.1 %all-reduce = (f32[48]{0:T(128)S(1)}, f32[48]{0:T(128)S(1)}) all-reduce(f32[48]{0:T(128)S(1)} %get-tuple-element.5, f32[48]{0:T(128)S(1)} %get-tuple-element.6), channel_id=1, replica_groups=mesh['gx'=8,'gy'=8,'gz'=8] {'gz'}, use_global_device_ids=true, to_apply=%region_10.0 | all-reduce | flops 96 | bytes 768 | tf_op jit(solution)/shard_map/psum | solution.py:77
  385.9 149.4 %psum.39 = f32[640]{0:T(1024)} all-reduce(f32[640]{0:T(1024)S(1)} %get-tuple-element.4), channel_id=1, replica_groups=mesh['gx'=8,'gy'=8,'gz'=8] {'gx','gy'}, use_global_device_ids=true, to_apply=%region_14.0 | all-reduce | flops 640 | bytes 5120 | tf_op jit(solution)/shard_map/psum | solution.py:75
  535.2 1.6 fusion.19
  (25 shorter events, 0.4 us)
Async XLA Ops:
  7.2 46.4 %all-gather.3.cloned.1.call-start = ((), (), s32[]{:S(2)}) async-start(), calls=%async_computation.5 | async-start | bytes 1290240 | tf_op jit(solution)/shard_map/all_gather | solution.py:34
  7.9 118.4 %all-gather.5.cloned.1.call-start = ((), (), s32[]{:S(2)}) async-start(), calls=%async_computation.7 | async-start | bytes 1290240 | tf_op jit(solution)/shard_map/all_gather | solution.py:23
  8.6 177.3 %reduce-scatter.6.cloned.1.call-start = ((), (), s32[]{:S(2)}) async-start(), calls=%async_computation.6 | async-start | bytes 774144 | tf_op jit(solution)/shard_map/reduce_scatter | solution.py:38
  35.7 20.8 %copy-start = (bf16[48,640]{1,0:T(8,128)(2,1)S(1)}, bf16[48,640]{1,0:T(8,128)(2,1)}, u32[]{:S(2)}) copy-start(bf16[48,640]{1,0:T(8,128)(2,1)} %param.5) | copy-start | bytes 184324
  35.7 68.0 %copy-start.1 = (f32[640]{0:T(1024)S(1)}, f32[640]{0:T(1024)}, u32[]{:S(2)}) copy-start(f32[640]{0:T(1024)} %param.6) | copy-start | bytes 7684
  56.4 217.8 %reduce-scatter.8.cloned.1.call-start = ((), (), s32[]{:S(2)}) async-start(), calls=%async_computation.8 | async-start | bytes 774144 | tf_op jit(solution)/shard_map/reduce_scatter | solution.py:26
  129.2 185.5 %copy-start.2 = (bf16[640,896]{1,0:T(8,128)(2,1)S(1)}, bf16[640,896]{1,0:T(8,128)(2,1)}, u32[]{:S(2)}) copy-start(bf16[640,896]{1,0:T(8,128)(2,1)} %all-gather.5.cloned.1.call-done) | copy-start | bytes 3440644
  129.2 232.5 %reduce-scatter.10.cloned.1.call-start = ((), (), s32[]{:S(2)}) async-start(), calls=%async_computation.9 | async-start | bytes 552960 | tf_op jit(solution)/shard_map/reduce_scatter | solution.py:67
  316.3 220.5 %reduce-scatter.14.cloned.1.call-start = ((), (), s32[]{:S(2)}) async-start(), calls=%async_computation.11 | async-start | bytes 1290240 | tf_op jit(solution)/shard_map/reduce_scatter | solution.py:49
  359.7 177.1 %reduce-scatter.12.cloned.1.call-start = ((), (), s32[]{:S(2)}) async-start(), calls=%async_computation.10 | async-start | bytes 1290240 | tf_op jit(solution)/shard_map/reduce_scatter | solution.py:58
Sparse Core Ops, SparseCore 0:
  10.1 43.4 all-gather.2
  55.6 39.0 all-gather.4
  99.2 86.6 reduce-scatter.5
  191.0 83.2 reduce-scatter.7
  316.5 40.0 reduce-scatter.9
  360.0 47.1 reduce-scatter.13
  410.9 39.1 reduce-scatter.11
where the time goes:
time: 544 us
  blocking collectives  350 us (64%)
  waiting for transfers between devices  164 us (30%)
  between operations  14.2 us (3%)
  matrix products  11.1 us (2%)
    psum x1, blocking collectives, body(): d_gain = lax.psum(jnp.sum(d_z * normed, axis=0), ('gx', 'gy'))  149 us
    reduce_scatter x1, waiting for transfers between devices, body(): lax.psum_scatter(jnp.dot(part_rows, up_full, preferred_element_type=jnp.f...  88.3 us
    reduce_scatter x1, waiting for transfers between devices, body(): lax.psum_scatter(lax.dot_general(part_rows, down_full, (((1,), (1,)), (()...  56.7 us
    all_gather x1, blocking collectives, body(): act_rows = lax.all_gather(act, 'gz', axis=0, tiled=True)  41.4 us
    all_gather x1, blocking collectives, body(): hgrad_rows = lax.all_gather(d_hidden, 'gz', axis=0, tiled=True)  39.4 us
    all_gather x1, blocking collectives, body(): out_rows = lax.all_gather(d_out, 'gx', axis=0, tiled=True)  27 us
    psum x1, blocking collectives, body(): total = lax.psum(jnp.sum(xf, axis=1), 'gz')  26.6 us
    psum x1, blocking collectives, body(): lax.psum((jnp.sum(d_scaled, axis=1), jnp.sum(d_scaled * normed, axis=1)),...  23.1 us
  transfers between devices with their start and end apart: 7, of which 3 were waited for; matrix products, arithmetic and copies ran while one was open for 2% of the time, Pallas kernels for 0%

commit v1 on v0

--- a/solution.py
+++ b/solution.py
@@ -72,7 +72,7 @@
         scatter_dimension=0,
         tiled=True,
     ).astype(jnp.float32)
-    d_gain = lax.psum(jnp.sum(d_z * normed, axis=0), ("gx", "gy"))
+    d_gain = lax.psum(lax.psum(jnp.sum(d_z * normed, axis=0), "gx"), "gy")
     d_scaled = d_z * gain
     scaled_sum, cross_sum = lax.psum(
         (jnp.sum(d_scaled, axis=1), jnp.sum(d_scaled * normed, axis=1)), "gz"

time: 544 us -> 459 us (0.84)
  blocking collectives: 350 us -> 247 us
  waiting for transfers between devices: 164 us -> 181 us
    psum x1 -> x2, blocking collectives: 149 us -> 46.2 us  [body(): d_gain = lax.psum(lax.psum(jnp.sum(d_z * normed, axis=0), 'gx'), 'gy')]
    reduce_scatter x1, waiting for transfers between devices: 0.01 us -> 16.6 us  [body(): lax.psum_scatter(lax.dot_general(columns, hgrad_rows, (((0,), (0,)), ((),...]
  transfers between devices with their start and end apart: 7 -> 7, of which waited for: 3 -> 4; matrix products, arithmetic and copies ran while one was open for 2% -> 3% of each run, Pallas kernels for 0% -> 0%
where the time goes in v1:
time: 459 us; the launch traced here: 457 us
  blocking collectives  247 us (54%)
  waiting for transfers between devices  181 us (39%)
  between operations  14.2 us (3%)
  matrix products  11.1 us (2%)
    reduce_scatter x1, waiting for transfers between devices, body(): lax.psum_scatter(jnp.dot(part_rows, up_full, preferred_element_type=jnp.f...  88.3 us
    reduce_scatter x1, waiting for transfers between devices, body(): lax.psum_scatter(lax.dot_general(part_rows, down_full, (((1,), (1,)), (()...  56.7 us
    psum x2, blocking collectives, body(): d_gain = lax.psum(lax.psum(jnp.sum(d_z * normed, axis=0), 'gx'), 'gy')  46.2 us
    all_gather x1, blocking collectives, body(): act_rows = lax.all_gather(act, 'gz', axis=0, tiled=True)  41.4 us
    all_gather x1, blocking collectives, body(): hgrad_rows = lax.all_gather(d_hidden, 'gz', axis=0, tiled=True)  39.4 us
    all_gather x1, blocking collectives, body(): out_rows = lax.all_gather(d_out, 'gx', axis=0, tiled=True)  27 us
    psum x1, blocking collectives, body(): total = lax.psum(jnp.sum(xf, axis=1), 'gz')  26.6 us
    psum x1, blocking collectives, body(): lax.psum((jnp.sum(d_scaled, axis=1), jnp.sum(d_scaled * normed, axis=1)),...  23.1 us
  transfers between devices with their start and end apart: 7, of which 4 were waited for; matrix products, arithmetic and copies ran while one was open for 3% of the time, Pallas kernels for 0%

profile of v1, /device:TPU:1, one launch (start us, length us, event | category | flops | bytes accessed | tf_op | source)
XLA Modules:
  0.0 457.1 jit_solution(13376105203539587591)
XLA Ops:
  7.2 0.7 all-gather.3.cloned.1.call-update
  7.9 0.7 all-gather.5.cloned.1.call-update
  8.7 27.0 %all_gather.18 = bf16[384,640]{1,0:T(8,128)(2,1)S(1)} all-gather(bf16[48,640]{1,0:T(8,128)(2,1)} %param.9), channel_id=1, replica_groups=mesh['gx'=8,'gy'=8,'gz'=8] {'gx'}, dimensions={0}, use_global_device_ids=true | all-gather | bytes 552960 | tf_op jit(solution)/shard_map/all_gather | solution.py:35
  35.7 17.8 %all-gather.3.cloned.1.call-done = bf16[896,640]{1,0:T(8,128)(2,1)} async-done(((bf16[112,640]{1,0:T(8,128)(2,1)}), bf16[896,640]{1,0:T(8,128)(2,1)}) %all-gather.3.cloned.1.call-update) | async-done | bytes 1146896 | tf_op jit(solution)/shard_map/all_gather | solution.py:34
  53.5 2.9 convolution_convert_fusion.3
  56.6 26.6 %psum.42 = f32[48]{0:T(128)S(1)} all-reduce(f32[48]{0:T(128)S(1)} %convert_reduce_fusion), channel_id=1, replica_groups=mesh['gx'=8,'gy'=8,'gz'=8] {'gz'}, use_global_device_ids=true, to_apply=%region_1.0 | all-reduce | flops 48 | bytes 384 | tf_op jit(solution)/shard_map/psum | solution.py:16
  83.2 0.2 fusion.20
  83.4 20.3 %psum.43 = f32[48]{0:T(128)S(1)} all-reduce(f32[48]{0:T(128)S(1)} %fusion.20), channel_id=1, replica_groups=mesh['gx'=8,'gy'=8,'gz'=8] {'gz'}, use_global_device_ids=true, to_apply=%region_3.0 | all-reduce | flops 48 | bytes 384 | tf_op jit(solution)/shard_map/psum | solution.py:19
  103.8 22.4 %all_gather.20 = bf16[384,640]{1,0:T(8,128)(2,1)S(1)} all-gather(bf16[48,640]{1,0:T(8,128)(2,1)S(1)} %fusion.16), channel_id=1, replica_groups=mesh['gx'=8,'gy'=8,'gz'=8] {'gx'}, dimensions={0}, use_global_device_ids=true | all-gather | bytes 552960 | tf_op jit(solution)/shard_map/all_gather | solution.py:24
  126.3 2.9 convolution_convert_fusion.2
  129.3 56.7 %reduce-scatter.6.cloned.1.call-done = bf16[48,896]{1,0:T(8,128)(2,1)} async-done(((bf16[384,896]{1,0:T(8,128)(2,1)}), bf16[48,896]{1,0:T(8,128)(2,1)}) %reduce-scatter.6.cloned.1.call-update) | async-done | bytes 86032 | tf_op jit(solution)/shard_map/reduce_scatter | solution.py:38
  185.9 88.3 %reduce-scatter.8.cloned.1.call-done = bf16[48,896]{1,0:T(8,128)(2,1)} async-done(((bf16[384,896]{1,0:T(8,128)(2,1)}), bf16[48,896]{1,0:T(8,128)(2,1)}) %reduce-scatter.8.cloned.1.call-update) | async-done | bytes 86032 | tf_op jit(solution)/shard_map/reduce_scatter | solution.py:26
  274.3 1.0 fusion.8
  275.3 39.4 %all_gather.22 = bf16[384,896]{1,0:T(8,128)(2,1)S(1)} all-gather(bf16[48,896]{1,0:T(8,128)(2,1)S(1)} %get-tuple-element.10), channel_id=1, replica_groups=mesh['gx'=8,'gy'=8,'gz'=8] {'gz'}, dimensions={0}, use_global_device_ids=true | all-gather | bytes 774144 | tf_op jit(solution)/shard_map/all_gather | solution.py:47
  314.7 1.6 convolution_convert_fusion.4
  316.4 41.4 %all_gather.23 = bf16[384,896]{1,0:T(8,128)(2,1)S(1)} all-gather(bf16[48,896]{1,0:T(8,128)(2,1)S(1)} %get-tuple-element.9), channel_id=1, replica_groups=mesh['gx'=8,'gy'=8,'gz'=8] {'gz'}, dimensions={0}, use_global_device_ids=true | all-gather | bytes 774144 | tf_op jit(solution)/shard_map/all_gather | solution.py:36
  357.8 1.9 convolution_convert_fusion
  359.8 1.9 convolution_convert_fusion.1
  361.7 1.0 fusion.22
  362.7 23.1 %all-reduce = (f32[48]{0:T(128)S(1)}, f32[48]{0:T(128)S(1)}) all-reduce(f32[48]{0:T(128)S(1)} %get-tuple-element.5, f32[48]{0:T(128)S(1)} %get-tuple-element.6), channel_id=1, replica_groups=mesh['gx'=8,'gy'=8,'gz'=8] {'gz'}, use_global_device_ids=true, to_apply=%region_10.0 | all-reduce | flops 96 | bytes 768 | tf_op jit(solution)/shard_map/psum | solution.py:77
  385.9 12.2 %psum.46 = f32[640]{0:T(1024)S(1)} all-reduce(f32[640]{0:T(1024)S(1)} %get-tuple-element.4), channel_id=1, replica_groups=mesh['gx'=8,'gy'=8,'gz'=8] {'gx'}, use_global_device_ids=true, to_apply=%region_14.0 | all-reduce | flops 640 | bytes 5120 | tf_op jit(solution)/shard_map/psum | solution.py:75
  398.1 34.0 %psum.47 = f32[640]{0:T(1024)} all-reduce(f32[640]{0:T(1024)S(1)} %psum.46), channel_id=1, replica_groups=mesh['gx'=8,'gy'=8,'gz'=8] {'gy'}, use_global_device_ids=true, to_apply=%region_15.0 | all-reduce | flops 640 | bytes 5120 | tf_op jit(solution)/shard_map/psum | solution.py:75
  432.0 1.6 fusion.19
  433.6 16.6 %reduce-scatter.12.cloned.1.call-done = bf16[80,896]{1,0:T(8,128)(2,1)} async-done(((bf16[640,896]{1,0:T(8,128)(2,1)}), bf16[80,896]{1,0:T(8,128)(2,1)}) %reduce-scatter.12.cloned.1.call-update) | async-done | bytes 143376 | tf_op jit(solution)/shard_map/reduce_scatter | solution.py:58
  (26 shorter events, 0.6 us)
Async XLA Ops:
  7.2 46.4 %all-gather.3.cloned.1.call-start = ((), (), s32[]{:S(2)}) async-start(), calls=%async_computation.5 | async-start | bytes 1290240 | tf_op jit(solution)/shard_map/all_gather | solution.py:34
  7.9 118.4 %all-gather.5.cloned.1.call-start = ((), (), s32[]{:S(2)}) async-start(), calls=%async_computation.7 | async-start | bytes 1290240 | tf_op jit(solution)/shard_map/all_gather | solution.py:23
  8.6 177.3 %reduce-scatter.6.cloned.1.call-start = ((), (), s32[]{:S(2)}) async-start(), calls=%async_computation.6 | async-start | bytes 774144 | tf_op jit(solution)/shard_map/reduce_scatter | solution.py:38
  35.7 20.8 %copy-start = (bf16[48,640]{1,0:T(8,128)(2,1)S(1)}, bf16[48,640]{1,0:T(8,128)(2,1)}, u32[]{:S(2)}) copy-start(bf16[48,640]{1,0:T(8,128)(2,1)} %param.5) | copy-start | bytes 184324
  35.7 68.0 %copy-start.1 = (f32[640]{0:T(1024)S(1)}, f32[640]{0:T(1024)}, u32[]{:S(2)}) copy-start(f32[640]{0:T(1024)} %param.6) | copy-start | bytes 7684
  56.4 217.8 %reduce-scatter.8.cloned.1.call-start = ((), (), s32[]{:S(2)}) async-start(), calls=%async_computation.8 | async-start | bytes 774144 | tf_op jit(solution)/shard_map/reduce_scatter | solution.py:26
  129.2 185.5 %copy-start.2 = (bf16[640,896]{1,0:T(8,128)(2,1)S(1)}, bf16[640,896]{1,0:T(8,128)(2,1)}, u32[]{:S(2)}) copy-start(bf16[640,896]{1,0:T(8,128)(2,1)} %all-gather.5.cloned.1.call-done) | copy-start | bytes 3440644
  129.2 232.5 %reduce-scatter.10.cloned.1.call-start = ((), (), s32[]{:S(2)}) async-start(), calls=%async_computation.9 | async-start | bytes 552960 | tf_op jit(solution)/shard_map/reduce_scatter | solution.py:67
  316.3 117.3 %reduce-scatter.14.cloned.1.call-start = ((), (), s32[]{:S(2)}) async-start(), calls=%async_computation.11 | async-start | bytes 1290240 | tf_op jit(solution)/shard_map/reduce_scatter | solution.py:49
  359.7 90.5 %reduce-scatter.12.cloned.1.call-start = ((), (), s32[]{:S(2)}) async-start(), calls=%async_computation.10 | async-start | bytes 1290240 | tf_op jit(solution)/shard_map/reduce_scatter | solution.py:58
Sparse Core Ops, SparseCore 0:
  10.1 43.4 all-gather.2
  55.6 39.0 all-gather.4
  99.2 86.6 reduce-scatter.5
  191.0 83.2 reduce-scatter.7
  316.5 40.0 reduce-scatter.9
  360.0 47.1 reduce-scatter.13
  410.9 39.2 reduce-scatter.11
